TPU v7x, 32 devices: a whole 2x2x4 slice. The times are simulated.
32 devices in a mesh: clip: 4 (over x, core), seq: 8 (over z, y).
Axes of the slice: x: 2, y: 2, z: 4, core: 2. Of those that a mesh axis runs over, the one named last changes fastest.
Arguments:
- video_query: bfloat16 [4096, 4096], P(('clip', 'seq')), parts along dimension 0
- video_key: bfloat16 [4096, 4096], P(('clip', 'seq')), parts along dimension 0
- video_value: bfloat16 [4096, 4096], P(('clip', 'seq')), parts along dimension 0, may hold values from -6 to 6
- cross_query: bfloat16 [4096, 4096], P(('clip', 'seq')), parts along dimension 0
- text_rows: bfloat16 [2048, 4096], P(('clip', 'seq')), parts along dimension 0, may hold values from -6 to 6
- text_block: int32 [32], P('clip'), parts along dimension 0, may hold values from 0 to 7, each once
- text_length: int32 [4], P('clip'), parts along dimension 0, may hold values from 64 to 512
- key_weight: bfloat16 [4096, 4096], P(None, 'seq'), may hold values from -0.09375 to 0.09375
- value_weight: bfloat16 [4096, 4096], P(None, 'seq'), may hold values from -0.09375 to 0.09375
Outputs:
- self_out: bfloat16 [4096, 4096], P(('clip', 'seq')), parts along dimension 0
- cross_out: bfloat16 [4096, 4096], P(('clip', 'seq')), parts along dimension 0
There are 4 independent parts, one for each index of `clip`. A program takes and returns all parts, laid end to end along the dimension named above; an argument that names none is the same for every part. Nothing has to cross between parts.
Inputs may be any that keep to these rules, and one draw needn't show every extreme that they name: A permutation: arrival block j holds prompt rows text_block[j] * 64 onward.
All inputs are finite; a program needn't handle non-finite values.
Results may differ from a plain program's by a relative error of at most 0.012.
The roundings to bfloat16 on the way count: a program that leaves them out, or rounds other values in their place, can miss the bound.
Values may be sent and summed in bfloat16 or wider, within the bound.
A program may use at most 128 MiB of HBM per device.

v0:
```python
import functools
import math

import jax
import jax.numpy as jnp
from jax import lax
from jax.experimental import pallas as pl
from jax.experimental.pallas import tpu as pltpu
from jax.sharding import PartitionSpec as P

HEAD_DIM = 128
MESH = pl.DeviceIdType.MESH
F32 = jnp.float32
BF16 = jnp.bfloat16
SCORE_SCALE = HEAD_DIM ** (-0.5) * math.log2(math.e)


def softmax_rows(scores, bias):
    scores = scores * SCORE_SCALE
    if bias is not None:
        scores = scores + bias
    highest = jnp.max(scores, axis=-1, keepdims=True)
    exponent = jnp.exp2(scores - highest)
    total = jnp.sum(exponent, axis=-1, keepdims=True)
    return (exponent * (1.0 / total)).astype(BF16)


def attend(query, key, value, bias, out, block):
    def one(step, carry):
        rows = pl.ds(pl.multiple_of(step * block, block), block)
        scores = lax.dot_general(
            query[rows, :], key[...], (((1,), (1,)), ((), ())), preferred_element_type=F32
        )
        weights = softmax_rows(scores, None if bias is None else bias[...])
        out[rows, :] = jnp.dot(weights, value[...], preferred_element_type=F32).astype(BF16)
        return carry

    lax.fori_loop(0, query.shape[0] // block, one, 0)


def kernel(
    n,
    lines,
    block_ref,
    length_ref,
    q_in,
    k_in,
    v_in,
    c_in,
    text_in,
    wk_in,
    wv_in,
    self_out,
    cross_out,
    q_buf,
    k_buf,
    v_buf,
    c_buf,
    so_buf,
    co_buf,
    text,
    wk,
    wv,
    tk,
    tv,
    bias,
    in_send,
    in_recv,
    out_send,
    out_recv,
    text_recv,
    up_send,
    down_send,
    side_send,
    w_sem,
):
    heads, tokens, dim = q_buf.shape
    own = tokens // n
    shard = text.shape[1]
    me = lax.axis_index("seq")
    side = n // lines
    pos = me // side
    lane = me % side

    def to(target):
        return {"seq": target}

    barrier = pltpu.get_barrier_semaphore()

    def greet(d, carry):
        pl.semaphore_signal(barrier, inc=1, device_id=to((me + d) % n), device_id_type=MESH)
        return carry

    w_copies = [
        pltpu.make_async_copy(wk_in, wk, w_sem.at[0]),
        pltpu.make_async_copy(wv_in, wv, w_sem.at[1]),
    ]
    own_text = pltpu.make_async_copy(text_in, text.at[me], text_recv.at[me])
    lax.fori_loop(1, n, greet, 0)
    own_text.start()
    pl.semaphore_wait(barrier, n - 1)

    ends = []

    def text_send(source, index, target, sem):
        return pltpu.make_async_remote_copy(
            src_ref=source,
            dst_ref=text.at[index],
            send_sem=sem,
            recv_sem=text_recv.at[index],
            device_id=to(target),
            device_id_type=MESH,
        )

    def forward(source, line, step, up, down):
        index = line * side + lane
        if up:
            copy_up = text_send(source, index, me + side, up_send.at[step])

            @pl.when(pos + 1 < lines)
            def _():
                copy_up.start()

        if down:
            copy_down = text_send(source, index, me - side, down_send.at[step])

            @pl.when(pos >= 1)
            def _():
                copy_down.start()

        for k in range(1, side):
            text_send(
                source, index, pos * side + (lane + k) % side, side_send.at[line, k]
            ).start()

    def text_wait(index):
        pltpu.make_async_copy(text.at[index], text.at[index], text_recv.at[index]).wait()

    def relay(step):
        @pl.when(pos >= step)
        def _():
            index = (pos - step) * side + lane
            text_wait(index)
            forward(text.at[index], pos - step, step, True, False)

        @pl.when(pos + step < lines)
        def _():
            index = (pos + step) * side + lane
            text_wait(index)
            forward(text.at[index], pos + step, step, False, True)

    arrays = ((q_in, q_buf), (k_in, k_buf), (v_in, v_buf), (c_in, c_buf))

    def columns(owner, h):
        return pl.ds(pl.multiple_of((owner * heads + h) * dim, dim), dim)

    def rows(owner):
        return pl.ds(pl.multiple_of(owner * own, own), own)

    def send_in(which, h):
        def one(d, carry):
            target = (me + d) % n
            for t in which:
                source, landing = arrays[t]
                pltpu.make_async_remote_copy(
                    src_ref=source.at[:, columns(target, h)],
                    dst_ref=landing.at[h, rows(me), :],
                    send_sem=in_send.at[t, h],
                    recv_sem=in_recv.at[t, h],
                    device_id=to(target),
                    device_id_type=MESH,
                ).start()
            return carry

        for t in which:
            source, landing = arrays[t]
            pltpu.make_async_copy(
                source.at[:, columns(me, h)], landing.at[h, rows(me), :], in_recv.at[t, h]
            ).start()
        lax.fori_loop(1, n, one, 0)

    def wait_in(which, h):
        for t in which:
            landing = arrays[t][1].at[h]
            pltpu.make_async_copy(landing, landing, in_recv.at[t, h]).wait()

    results = ((so_buf, self_out), (co_buf, cross_out))

    def send_out(t, h):
        source, landing = results[t]

        def one(d, carry):
            target = (me + d) % n
            pltpu.make_async_remote_copy(
                src_ref=source.at[h, rows(target), :],
                dst_ref=landing.at[:, columns(me, h)],
                send_sem=out_send.at[t, h],
                recv_sem=out_recv.at[t],
                device_id=to(target),
                device_id_type=MESH,
            ).start()
            return carry

        lax.fori_loop(1, n, one, 0)
        pltpu.make_async_copy(
            source.at[h, rows(me), :], landing.at[:, columns(me, h)], out_recv.at[t]
        ).start()

    block = math.gcd(tokens, 256)

    def self_head(h):
        wait_in((0, 1, 2), h)
        attend(q_buf.at[h], k_buf.at[h], v_buf.at[h], None, so_buf.at[h], block)
        send_out(0, h)

    forward(text_in, pos, 0, True, True)
    send_in((0, 1, 2), 0)
    for copy in w_copies:
        copy.start()
    for step in range(1, max(lines, heads)):
        if step < lines:
            relay(step)
        if step < heads:
            send_in((0, 1, 2), step)
        if step == lines - 1 or (step == heads - 1 and heads > lines):
            for h in range(heads):
                send_in((3,), h)
        if step <= heads:
            self_head(step - 1)
    for h in range(max(lines, heads) - 1, heads):
        self_head(h)

    text_wait(me)
    for line in range(lines):
        for k in range(1, side):
            text_wait(line * side + (lane + k) % side)
    for copy in w_copies:
        copy.wait()

    text_rows = n * shard
    flat = text.reshape(text_rows, text.shape[2])
    tall = math.gcd(text_rows, 256)
    wide = math.gcd(wk.shape[1], 256)
    across = wk.shape[1] // wide

    def project(step, carry):
        r = pl.ds(pl.multiple_of((step // across) * tall, tall), tall)
        c = pl.ds(pl.multiple_of((step % across) * wide, wide), wide)
        tk[r, c] = jnp.dot(flat[r, :], wk[:, c], preferred_element_type=F32).astype(BF16)
        tv[r, c] = jnp.dot(flat[r, :], wv[:, c], preferred_element_type=F32).astype(BF16)
        return carry

    lax.fori_loop(0, (text_rows // tall) * across, project, 0)

    arrival = lax.broadcasted_iota(jnp.int32, bias.shape, 1)
    limit = jnp.zeros(bias.shape, jnp.int32)
    for j in range(n):
        held = length_ref[0] - block_ref[j] * shard
        limit = jnp.where(arrival // shard == j, held, limit)
    bias[...] = jnp.where(arrival % shard < limit, 0.0, -jnp.inf).astype(F32)

    for h in range(heads):
        c = slice(h * dim, (h + 1) * dim)
        wait_in((3,), h)
        attend(c_buf.at[h], tk.at[:, c], tv.at[:, c], bias, co_buf.at[h], block)
        send_out(1, h)

    for t in range(4):
        landing = arrays[t][1]
        for h in range(heads):
            part = landing.at[h, pl.ds(0, (n - 1) * own), :]
            pltpu.make_async_copy(part, part, in_send.at[t, h]).wait()
    for t in range(2):
        source, landing = results[t]
        for h in range(heads):
            part = source.at[h, pl.ds(0, (n - 1) * own), :]
            pltpu.make_async_copy(part, part, out_send.at[t, h]).wait()
        pltpu.make_async_copy(landing, landing, out_recv.at[t]).wait()

    for step in range(lines):
        up = text_send(text_in, me, me, up_send.at[step])
        down = text_send(text_in, me, me, down_send.at[step])

        @pl.when(jnp.logical_and(pos + 1 < lines, pos >= step))
        def _():
            up.wait_send()

        @pl.when(jnp.logical_and(pos >= 1, pos + step < lines))
        def _():
            down.wait_send()

        for k in range(1, side):
            text_send(text_in, me, me, side_send.at[step, k]).wait_send()


def settle_kernel(a, b, a_out, b_out, sem):
    copies = [
        pltpu.make_async_copy(a, a_out, sem.at[0]),
        pltpu.make_async_copy(b, b_out, sem.at[1]),
    ]
    for copy in copies:
        copy.start()
    for copy in copies:
        copy.wait()


def settle(pair):
    any_spec = pl.BlockSpec(memory_space=pl.ANY)
    return tuple(
        pl.pallas_call(
            settle_kernel,
            name="settle",
            out_shape=[pltpu.HBM(x.shape, x.dtype) for x in pair],
            in_specs=[any_spec] * 2,
            out_specs=[any_spec] * 2,
            scratch_shapes=[pltpu.SemaphoreType.DMA((2,))],
            compiler_params=pltpu.CompilerParams(vmem_limit_bytes=1024 * 1024),
        )(*pair)
    )


def body(
    video_query,
    video_key,
    video_value,
    cross_query,
    text_rows,
    text_block,
    text_length,
    key_weight,
    value_weight,
):
    n = lax.axis_size("seq")
    lines = 4 if n % 4 == 0 else n
    own, inner = video_query.shape
    shard, d_text = text_rows.shape
    width = key_weight.shape[1]
    heads = width // HEAD_DIM
    tokens = own * n
    any_spec = pl.BlockSpec(memory_space=pl.ANY)
    smem_spec = pl.BlockSpec(memory_space=pltpu.SMEM)
    head_buf = pltpu.VMEM((heads, tokens, HEAD_DIM), BF16)
    dma = pltpu.SemaphoreType.DMA
    return settle(
        pl.pallas_call(
            functools.partial(kernel, n, lines),
            name="video_block",
            out_shape=[pltpu.VMEM((own, inner), BF16)] * 2,
            in_specs=[smem_spec] * 2 + [any_spec] * 7,
            out_specs=[any_spec] * 2,
            scratch_shapes=[head_buf] * 6
            + [
                pltpu.VMEM((n, shard, d_text), BF16),
                pltpu.VMEM((d_text, width), BF16),
                pltpu.VMEM((d_text, width), BF16),
                pltpu.VMEM((n * shard, width), BF16),
                pltpu.VMEM((n * shard, width), BF16),
                pltpu.VMEM((1, n * shard), F32),
                dma((4, heads)),
                dma((4, heads)),
                dma((2, heads)),
                dma((2,)),
                dma((n,)),
                dma((lines,)),
                dma((lines,)),
                dma((lines, max(n // lines, 2))),
                dma((2,)),
            ],
            compiler_params=pltpu.CompilerParams(
                collective_id=0, has_side_effects=True, vmem_limit_bytes=58 * 1024 * 1024
            ),
        )(
            text_block,
            text_length,
            video_query,
            video_key,
            video_value,
            cross_query,
            text_rows,
            key_weight,
            value_weight,
        )
    )


def solution(mesh):
    return jax.shard_map(
        body,
        mesh=mesh,
        in_specs=(
            P(("clip", "seq"), None),
            P(("clip", "seq"), None),
            P(("clip", "seq"), None),
            P(("clip", "seq"), None),
            P(("clip", "seq"), None),
            P("clip"),
            P("clip"),
            P(None, "seq"),
            P(None, "seq"),
        ),
        out_specs=(P(("clip", "seq"), None), P(("clip", "seq"), None)),
        check_vma=False,
    )
```

profile of v0, /device:TPU:12, one launch (start us, length us, event | category | flops | bytes accessed | tf_op | source)
XLA Modules:
  0.0 166.2 jit_solution(2028464194673719924)
XLA Ops:
  1.3 163.6 %video_block.1 = (bf16[128,4096]{1,0:T(8,128)(2,1)S(1)}, bf16[128,4096]{1,0:T(8,128)(2,1)S(1)}) custom-call(s32[8]{0:T(128)} %block_ref.1, s32[1]{0:T(128)S(6)} %copy.11.length_ref, bf16[128,4096]{1,0:T(8,128)(2,1)} %q_in.1, bf16[128,4096]{1,0:T(8,128)(2,1)} %k_in.1, bf16[128,4096]{1,0:T(8,128)(2,1)} %v_in.1, bf16[128,4096]{1,0:T(8,128)(2,1)} %c_in.1, ...), custom_call_target="tpu_custom_call" | custom-call | tf_op jit(solution)/shard_map/video_block/pallas_call | solution.py:345
  164.9 1.3 settle.1
where the time goes:
time: 168 us; the launch traced here: 166 us
  Pallas kernels  165 us (98%)
    pallas_call x1, Pallas kernels, body(): pl.pallas_call(functools.partial(kernel, n, lines), name='video_block', o...  164 us

commit v1 on v0

--- a/solution.py
+++ b/solution.py
@@ -41,8 +41,8 @@
 def kernel(
     n,
     lines,
-    block_ref,
-    length_ref,
+    block_in,
+    length_in,
     q_in,
     k_in,
     v_in,
@@ -64,6 +64,8 @@
     tk,
     tv,
     bias,
+    block_ref,
+    length_ref,
     in_send,
     in_recv,
     out_send,
@@ -73,6 +75,8 @@
     down_send,
     side_send,
     w_sem,
+    small_sem,
+    ready,
 ):
     heads, tokens, dim = q_buf.shape
     own = tokens // n
@@ -87,20 +91,21 @@
 
     barrier = pltpu.get_barrier_semaphore()
 
-    def greet(d, carry):
-        pl.semaphore_signal(barrier, inc=1, device_id=to((me + d) % n), device_id_type=MESH)
-        return carry
-
     w_copies = [
         pltpu.make_async_copy(wk_in, wk, w_sem.at[0]),
         pltpu.make_async_copy(wv_in, wv, w_sem.at[1]),
     ]
+    small_copies = [
+        pltpu.make_async_copy(block_in, block_ref, small_sem.at[0]),
+        pltpu.make_async_copy(length_in, length_ref, small_sem.at[1]),
+    ]
     own_text = pltpu.make_async_copy(text_in, text.at[me], text_recv.at[me])
-    lax.fori_loop(1, n, greet, 0)
     own_text.start()
-    pl.semaphore_wait(barrier, n - 1)
-
-    ends = []
+
+    low = lines // 2 - 1
+    high = low + 1
+    middle = jnp.logical_or(pos == low, pos == high)
+    outer_lines = [line for line in range(lines) if line not in (low, high)]
 
     def text_send(source, index, target, sem):
         return pltpu.make_async_remote_copy(
@@ -112,22 +117,22 @@
             device_id_type=MESH,
         )
 
-    def forward(source, line, step, up, down):
+    def forward_up(source, line, step):
+        copy = text_send(source, line * side + lane, me + side, up_send.at[step])
+
+        @pl.when(pos + 1 < lines)
+        def _():
+            copy.start()
+
+    def forward_down(source, line, step):
+        copy = text_send(source, line * side + lane, me - side, down_send.at[step])
+
+        @pl.when(pos >= 1)
+        def _():
+            copy.start()
+
+    def forward_side(source, line):
         index = line * side + lane
-        if up:
-            copy_up = text_send(source, index, me + side, up_send.at[step])
-
-            @pl.when(pos + 1 < lines)
-            def _():
-                copy_up.start()
-
-        if down:
-            copy_down = text_send(source, index, me - side, down_send.at[step])
-
-            @pl.when(pos >= 1)
-            def _():
-                copy_down.start()
-
         for k in range(1, side):
             text_send(
                 source, index, pos * side + (lane + k) % side, side_send.at[line, k]
@@ -141,13 +146,15 @@
         def _():
             index = (pos - step) * side + lane
             text_wait(index)
-            forward(text.at[index], pos - step, step, True, False)
+            forward_up(text.at[index], pos - step, step)
+            forward_side(text.at[index], pos - step)
 
         @pl.when(pos + step < lines)
         def _():
             index = (pos + step) * side + lane
             text_wait(index)
-            forward(text.at[index], pos + step, step, False, True)
+            forward_down(text.at[index], pos + step, step)
+            forward_side(text.at[index], pos + step)
 
     arrays = ((q_in, q_buf), (k_in, k_buf), (v_in, v_buf), (c_in, c_buf))
 
@@ -213,9 +220,56 @@
         attend(q_buf.at[h], k_buf.at[h], v_buf.at[h], None, so_buf.at[h], block)
         send_out(0, h)
 
-    forward(text_in, pos, 0, True, True)
+    def hail(sem, line, lane_of):
+        pl.semaphore_signal(
+            sem, inc=1, device_id=to(line * side + lane_of), device_id_type=MESH
+        )
+
+    @pl.when(middle)
+    def _():
+        hail(barrier, low + high - pos, lane)
+        pl.semaphore_wait(barrier, 1)
+
+        @pl.when(pos == low)
+        def _():
+            forward_up(text_in, pos, 0)
+
+        @pl.when(pos == high)
+        def _():
+            forward_down(text_in, pos, 0)
+
+        for line in outer_lines:
+            for k in range(side):
+                hail(barrier, line, k)
+        pl.semaphore_wait(barrier, len(outer_lines) * side)
+
+        @pl.when(pos == low)
+        def _():
+            for line in outer_lines:
+                if line < low:
+                    hail(ready, line, lane)
+            forward_down(text_in, pos, 0)
+
+        @pl.when(pos == high)
+        def _():
+            for line in outer_lines:
+                if line > high:
+                    hail(ready, line, lane)
+            forward_up(text_in, pos, 0)
+
+    @pl.when(jnp.logical_not(middle))
+    def _():
+        pl.semaphore_wait(barrier, 2 * side)
+        for line in (low, high):
+            for k in range(side):
+                hail(barrier, line, k)
+        pl.semaphore_wait(ready, 1)
+        forward_up(text_in, pos, 0)
+        forward_down(text_in, pos, 0)
+
+    forward_side(text_in, pos)
     send_in((0, 1, 2), 0)
-    for copy in w_copies:
+    for copy in w_copies + small_copies:
         copy.start()
     for step in range(1, max(lines, heads)):
         if step < lines:
@@ -234,7 +288,7 @@
     for line in range(lines):
         for k in range(1, side):
             text_wait(line * side + (lane + k) % side)
-    for copy in w_copies:
+    for copy in w_copies + small_copies:
         copy.wait()
 
     text_rows = n * shard
@@ -338,7 +392,6 @@
     heads = width // HEAD_DIM
     tokens = own * n
     any_spec = pl.BlockSpec(memory_space=pl.ANY)
-    smem_spec = pl.BlockSpec(memory_space=pltpu.SMEM)
     head_buf = pltpu.VMEM((heads, tokens, HEAD_DIM), BF16)
     dma = pltpu.SemaphoreType.DMA
     return settle(
@@ -346,7 +399,7 @@
             functools.partial(kernel, n, lines),
             name="video_block",
             out_shape=[pltpu.VMEM((own, inner), BF16)] * 2,
-            in_specs=[smem_spec] * 2 + [any_spec] * 7,
+            in_specs=[any_spec] * 9,
             out_specs=[any_spec] * 2,
             scratch_shapes=[head_buf] * 6
             + [
@@ -356,6 +409,8 @@
                 pltpu.VMEM((n * shard, width), BF16),
                 pltpu.VMEM((n * shard, width), BF16),
                 pltpu.VMEM((1, n * shard), F32),
+                pltpu.SMEM((n,), jnp.int32),
+                pltpu.SMEM((1,), jnp.int32),
                 dma((4, heads)),
                 dma((4, heads)),
                 dma((2, heads)),
@@ -365,6 +420,8 @@
                 dma((lines,)),
                 dma((lines, max(n // lines, 2))),
                 dma((2,)),
+                dma((2,)),
+                pltpu.SemaphoreType.REGULAR,
             ],
             compiler_params=pltpu.CompilerParams(
                 collective_id=0, has_side_effects=True, vmem_limit_bytes=58 * 1024 * 1024

time: 168 us -> 166 us (0.988)
  Pallas kernels: 165 us -> 162 us
    pallas_call x1, Pallas kernels: 164 us -> 161 us  [body(): pl.pallas_call(functools.partial(kernel, n, lines), name='video_block', o...]
where the time goes in v1:
time: 166 us; the launch traced here: 163 us
  Pallas kernels  162 us (98%)
    pallas_call x1, Pallas kernels, body(): pl.pallas_call(functools.partial(kernel, n, lines), name='video_block', o...  161 us

profile of v1, /device:TPU:12, one launch (start us, length us, event | category | flops | bytes accessed | tf_op | source)
XLA Modules:
  0.0 163.5 jit_solution(1553274085631122998)
XLA Ops:
  1.3 160.9 %video_block.1 = (bf16[128,4096]{1,0:T(8,128)(2,1)S(1)}, bf16[128,4096]{1,0:T(8,128)(2,1)S(1)}) custom-call(s32[8]{0:T(128)} %block_in.1, s32[1]{0:T(128)S(6)} %copy.11.length_in, bf16[128,4096]{1,0:T(8,128)(2,1)} %q_in.1, bf16[128,4096]{1,0:T(8,128)(2,1)} %k_in.1, bf16[128,4096]{1,0:T(8,128)(2,1)} %v_in.1, bf16[128,4096]{1,0:T(8,128)(2,1)} %c_in.1, ...), custom_call_target="tpu_custom_call" | custom-call | tf_op jit(solution)/shard_map/video_block/pallas_call | solution.py:398
  162.2 1.3 settle.1

commit v2 on v1

--- a/solution.py
+++ b/solution.py
@@ -193,11 +193,15 @@
 
     results = ((so_buf, self_out), (co_buf, cross_out))
 
-    def send_out(t, h):
+    def send_out(t, h, parity):
         source, landing = results[t]
+        half = n // 2
+        mine = (pos // 2) * side + lane
+        same = pos % 2 == parity
 
         def one(d, carry):
-            target = (me + d) % n
+            slot = (mine + d) % half
+            target = (slot // side * 2 + parity) * side + slot % side
             pltpu.make_async_remote_copy(
                 src_ref=source.at[h, rows(target), :],
                 dst_ref=landing.at[:, columns(me, h)],
@@ -208,17 +212,21 @@
             ).start()
             return carry
 
-        lax.fori_loop(1, n, one, 0)
-        pltpu.make_async_copy(
-            source.at[h, rows(me), :], landing.at[:, columns(me, h)], out_recv.at[t]
-        ).start()
+        lax.fori_loop(jnp.where(same, 1, 0), half, one, 0)
+
+        @pl.when(same)
+        def _():
+            pltpu.make_async_copy(
+                source.at[h, rows(me), :], landing.at[:, columns(me, h)], out_recv.at[t]
+            ).start()
 
     block = math.gcd(tokens, 256)
 
     def self_head(h):
         wait_in((0, 1, 2), h)
         attend(q_buf.at[h], k_buf.at[h], v_buf.at[h], None, so_buf.at[h], block)
-        send_out(0, h)
+        send_out(0, h, 0)
+        send_out(0, h, 1)
 
     def hail(sem, line, lane_of):
         pl.semaphore_signal(
@@ -317,7 +325,11 @@
         c = slice(h * dim, (h + 1) * dim)
         wait_in((3,), h)
         attend(c_buf.at[h], tk.at[:, c], tv.at[:, c], bias, co_buf.at[h], block)
-        send_out(1, h)
+        send_out(1, h, 0)
+        if h < heads - 4:
+            send_out(1, h, 1)
+    for h in range(max(heads - 4, 0), heads):
+        send_out(1, h, 1)
 
     for t in range(4):
         landing = arrays[t][1]

time: 166 us -> 164 us (0.988); the launches traced: 163 us -> 164 us
  no operation moved by 1% of the time
where the time goes in v2:
time: 164 us
  Pallas kernels  162 us (99%)
    pallas_call x1, Pallas kernels, body(): pl.pallas_call(functools.partial(kernel, n, lines), name='video_block', o...  161 us

profile of v2, /device:TPU:12, one launch (start us, length us, event | category | flops | bytes accessed | tf_op | source)
XLA Modules:
  0.0 163.5 jit_solution(2977180779905984566)
XLA Ops:
  1.3 160.9 %video_block.1 = (bf16[128,4096]{1,0:T(8,128)(2,1)S(1)}, bf16[128,4096]{1,0:T(8,128)(2,1)S(1)}) custom-call(s32[8]{0:T(128)} %block_in.1, s32[1]{0:T(128)S(6)} %copy.11.length_in, bf16[128,4096]{1,0:T(8,128)(2,1)} %q_in.1, bf16[128,4096]{1,0:T(8,128)(2,1)} %k_in.1, bf16[128,4096]{1,0:T(8,128)(2,1)} %v_in.1, bf16[128,4096]{1,0:T(8,128)(2,1)} %c_in.1, ...), custom_call_target="tpu_custom_call" | custom-call | tf_op jit(solution)/shard_map/video_block/pallas_call | solution.py:410
  162.2 1.3 settle.1

commit v3 on v1

v3 whole, which is shorter than its diff:
```python
import functools
import math

import jax
import jax.numpy as jnp
from jax import lax
from jax.experimental import pallas as pl
from jax.experimental.pallas import tpu as pltpu
from jax.sharding import PartitionSpec as P

HEAD_DIM = 128
MESH = pl.DeviceIdType.MESH
F32 = jnp.float32
BF16 = jnp.bfloat16
SCORE_SCALE = HEAD_DIM ** (-0.5) * math.log2(math.e)


def softmax_rows(scores, bias):
    scores = scores * SCORE_SCALE
    if bias is not None:
        scores = scores + bias
    highest = jnp.max(scores, axis=-1, keepdims=True)
    exponent = jnp.exp2(scores - highest)
    total = jnp.sum(exponent, axis=-1, keepdims=True)
    return (exponent * (1.0 / total)).astype(BF16)


def attend(query, key, value, bias, out, block):
    def one(step, carry):
        rows = pl.ds(pl.multiple_of(step * block, block), block)
        scores = lax.dot_general(
            query[rows, :], key[...], (((1,), (1,)), ((), ())), preferred_element_type=F32
        )
        weights = softmax_rows(scores, None if bias is None else bias[...])
        out[rows, :] = jnp.dot(weights, value[...], preferred_element_type=F32).astype(BF16)
        return carry

    lax.fori_loop(0, query.shape[0] // block, one, 0)


def kernel(
    n,
    lines,
    block_in,
    length_in,
    q_in,
    k_in,
    v_in,
    c_in,
    text_in,
    wk_in,
    wv_in,
    self_out,
    cross_out,
    taken,
    made,
    text,
    weights,
    tk,
    tv,
    bias,
    block_ref,
    length_ref,
    in_send,
    qkv_recv,
    c_recv,
    out_send,
    out_recv,
    line_recv,
    side_recv,
    line_send,
    side_send,
    w_sem,
    small_sem,
    ready,
):
    heads, _, tokens, dim = taken.shape
    own = tokens // n
    shard = text.shape[1]
    me = lax.axis_index("seq")
    side = n // lines
    split = lines // 2
    low, high = split - 1, split
    outer_lines = [line for line in range(lines) if line not in (low, high)]
    pos = me // side
    lane = me % side
    middle = jnp.logical_or(pos == low, pos == high)

    def to(target):
        return {"seq": target}

    def far(target):
        return target // side // split != pos // split

    barrier = pltpu.get_barrier_semaphore()

    def hail(sem, line, lane_of):
        pl.semaphore_signal(
            sem, inc=1, device_id=to(line * side + lane_of), device_id_type=MESH
        )

    loads = [
        pltpu.make_async_copy(wk_in, weights.at[0], w_sem),
        pltpu.make_async_copy(wv_in, weights.at[1], w_sem),
        pltpu.make_async_copy(block_in, block_ref, small_sem.at[0]),
        pltpu.make_async_copy(length_in, length_ref, small_sem.at[1]),
    ]
    own_text = pltpu.make_async_copy(text_in, text.at[me], line_recv.at[pos])

    def text_send(source, index, target, sem, recv):
        return pltpu.make_async_remote_copy(
            src_ref=source,
            dst_ref=text.at[index],
            send_sem=sem,
            recv_sem=recv,
            device_id=to(target),
            device_id_type=MESH,
        )

    def forward_up(source, line):
        copy = text_send(source, line * side + lane, me + side, line_send, line_recv.at[line])

        @pl.when(pos + 1 < lines)
        def _():
            copy.start()

    def forward_down(source, line):
        copy = text_send(source, line * side + lane, me - side, line_send, line_recv.at[line])

        @pl.when(pos >= 1)
        def _():
            copy.start()

    def forward_side(source, line):
        for k in range(1, side):
            target = pos * side + (lane + k) % side
            text_send(source, line * side + lane, target, side_send, side_recv).start()

    def line_wait(line):
        shard_ref = text.at[line * side + lane]
        pltpu.make_async_copy(shard_ref, shard_ref, line_recv.at[line]).wait()

    def relay(step):
        @pl.when(pos >= step)
        def _():
            line = pos - step
            source = text.at[line * side + lane]
            line_wait(line)
            forward_up(source, line)
            forward_side(source, line)

        @pl.when(pos + step < lines)
        def _():
            line = pos + step
            source = text.at[line * side + lane]
            line_wait(line)
            forward_down(source, line)
            forward_side(source, line)

    sources = (q_in, k_in, v_in, c_in)

    def columns(owner, h):
        return pl.ds(pl.multiple_of((owner * heads + h) * dim, dim), dim)

    def rows(owner):
        return pl.ds(pl.multiple_of(owner * own, own), own)

    def send_in(which, h, recv):
        def one(d, carry):
            target = (me + d) % n
            for t in which:
                pltpu.make_async_remote_copy(
                    src_ref=sources[t].at[:, columns(target, h)],
                    dst_ref=taken.at[h, t, rows(me), :],
                    send_sem=in_send,
                    recv_sem=recv.at[h],
                    device_id=to(target),
                    device_id_type=MESH,
                ).start()
            return carry

        for t in which:
            pltpu.make_async_copy(
                sources[t].at[:, columns(me, h)], taken.at[h, t, rows(me), :], recv.at[h]
            ).start()
        lax.fori_loop(1, n, one, 0)

    results = (self_out, cross_out)

    def send_out(t, h, late):
        source, landing = made.at[t, h], results[t]

        def one(d, carry):
            target = (me + d) % n
            last = jnp.logical_and(far(target), target // side % 2 == 1)

            @pl.when(last if late else jnp.logical_not(last))
            def _():
                pltpu.make_async_remote_copy(
                    src_ref=source.at[rows(target), :],
                    dst_ref=landing.at[:, columns(me, h)],
                    send_sem=out_send,
                    recv_sem=out_recv.at[t],
                    device_id=to(target),
                    device_id_type=MESH,
                ).start()

            return carry

        lax.fori_loop(1, n, one, 0)
        if not late:
            pltpu.make_async_copy(
                source.at[rows(me), :], landing.at[:, columns(me, h)], out_recv.at[t]
            ).start()

    block = math.gcd(tokens, 256)

    def self_head(h):
        arrived = taken.at[h, pl.ds(0, 3)]
        pltpu.make_async_copy(arrived, arrived, qkv_recv.at[h]).wait()
        attend(taken.at[h, 0], taken.at[h, 1], taken.at[h, 2], None, made.at[0, h], block)
        send_out(0, h, False)
        send_out(0, h, True)

    @pl.when(middle)
    def _():
        hail(barrier, low + high - pos, lane)
        own_text.start()
        pl.semaphore_wait(barrier, 1)

        @pl.when(pos == low)
        def _():
            forward_up(text_in, pos)

        @pl.when(pos == high)
        def _():
            forward_down(text_in, pos)

        for line in outer_lines:
            for k in range(side):
                hail(barrier, line, k)
        pl.semaphore_wait(barrier, len(outer_lines) * side)

        @pl.when(pos == low)
        def _():
            for line in outer_lines:
                if line < low:
                    hail(ready, line, lane)
            forward_down(text_in, pos)

        @pl.when(pos == high)
        def _():
            for line in outer_lines:
                if line > high:
                    hail(ready, line, lane)
            forward_up(text_in, pos)

    @pl.when(jnp.logical_not(middle))
    def _():
        own_text.start()
        pl.semaphore_wait(barrier, 2 * side)
        for line in (low, high):
            for k in range(side):
                hail(barrier, line, k)
        pl.semaphore_wait(ready, 1)
        forward_up(text_in, pos)
        forward_down(text_in, pos)

    forward_side(text_in, pos)
    send_in((0, 1, 2), 0, qkv_recv)
    for copy in loads:
        copy.start()
    for step in range(1, max(lines, heads)):
        if step < lines:
            relay(step)
        if step < heads:
            send_in((0, 1, 2), step, qkv_recv)
        if step == lines - 1 or (step == heads - 1 and heads > lines):
            for h in range(heads):
                send_in((3,), h, c_recv)
        if step <= heads:
            self_head(step - 1)
    for h in range(max(lines, heads) - 1, heads):
        self_head(h)

    line_wait(pos)
    if side > 1:
        others = text.at[pl.ds(0, n - lines)]
        pltpu.make_async_copy(others, others, side_recv).wait()
    pltpu.make_async_copy(weights, weights, w_sem).wait()
    for copy in loads[2:]:
        copy.wait()

    text_rows = n * shard
    flat = text.reshape(text_rows, text.shape[2])
    width = weights.shape[2]
    tall = math.gcd(text_rows, 256)
    wide = math.gcd(width, 256)
    across = width // wide

    def project(step, carry):
        r = pl.ds(pl.multiple_of((step // across) * tall, tall), tall)
        c = pl.ds(pl.multiple_of((step % across) * wide, wide), wide)
        for which, out in ((0, tk), (1, tv)):
            out[r, c] = jnp.dot(
                flat[r, :], weights[which, :, c], preferred_element_type=F32
            ).astype(BF16)
        return carry

    lax.fori_loop(0, (text_rows // tall) * across, project, 0)

    arrival = lax.broadcasted_iota(jnp.int32, bias.shape, 1)
    limit = jnp.zeros(bias.shape, jnp.int32)
    for j in range(n):
        held = length_ref[0] - block_ref[j] * shard
        limit = jnp.where(arrival // shard == j, held, limit)
    bias[...] = jnp.where(arrival % shard < limit, 0.0, -jnp.inf).astype(F32)

    for h in range(heads):
        c = slice(h * dim, (h + 1) * dim)
        arrived = taken.at[h, 3]
        pltpu.make_async_copy(arrived, arrived, c_recv.at[h]).wait()
        attend(arrived, tk.at[:, c], tv.at[:, c], bias, made.at[1, h], block)
        send_out(1, h, False)
    for h in range(heads):
        send_out(1, h, True)

    away = pl.ds(0, (n - 1) * own)
    part = taken.at[:, :, away, :]
    pltpu.make_async_copy(part, part, in_send).wait()
    for p in range(lines):
        sent = (p + 1) * (p + 1 < lines) + (lines - p) * (p >= 1)

        @pl.when(pos == p)
        def _():
            part = text.at[pl.ds(0, sent)]
            pltpu.make_async_copy(part, part, line_send).wait()

    if side > 1:
        others = text.at[pl.ds(0, n - lines)]
        pltpu.make_async_copy(others, others, side_send).wait()
    part = made.at[:, :, away, :]
    pltpu.make_async_copy(part, part, out_send).wait()
    for t in range(2):
        pltpu.make_async_copy(results[t], results[t], out_recv.at[t]).wait()


def settle_kernel(a, b, a_out, b_out, sem):
    copies = [
        pltpu.make_async_copy(a, a_out, sem.at[0]),
        pltpu.make_async_copy(b, b_out, sem.at[1]),
    ]
    for copy in copies:
        copy.start()
    for copy in copies:
        copy.wait()


def settle(pair):
    any_spec = pl.BlockSpec(memory_space=pl.ANY)
    return tuple(
        pl.pallas_call(
            settle_kernel,
            name="settle",
            out_shape=[pltpu.HBM(x.shape, x.dtype) for x in pair],
            in_specs=[any_spec] * 2,
            out_specs=[any_spec] * 2,
            scratch_shapes=[pltpu.SemaphoreType.DMA((2,))],
            compiler_params=pltpu.CompilerParams(vmem_limit_bytes=1024 * 1024),
        )(*pair)
    )


def body(
    video_query,
    video_key,
    video_value,
    cross_query,
    text_rows,
    text_block,
    text_length,
    key_weight,
    value_weight,
):
    n = lax.axis_size("seq")
    lines = 4 if n % 4 == 0 else n
    own, inner = video_query.shape
    shard, d_text = text_rows.shape
    width = key_weight.shape[1]
    heads = width // HEAD_DIM
    tokens = own * n
    any_spec = pl.BlockSpec(memory_space=pl.ANY)
    dma = pltpu.SemaphoreType.DMA
    return settle(
        pl.pallas_call(
            functools.partial(kernel, n, lines),
            name="video_block",
            out_shape=[pltpu.VMEM((own, inner), BF16)] * 2,
            in_specs=[any_spec] * 9,
            out_specs=[any_spec] * 2,
            scratch_shapes=[
                pltpu.VMEM((heads, 4, tokens, HEAD_DIM), BF16),
                pltpu.VMEM((2, heads, tokens, HEAD_DIM), BF16),
                pltpu.VMEM((n, shard, d_text), BF16),
                pltpu.VMEM((2, d_text, width), BF16),
                pltpu.VMEM((n * shard, width), BF16),
                pltpu.VMEM((n * shard, width), BF16),
                pltpu.VMEM((1, n * shard), F32),
                pltpu.SMEM((n,), jnp.int32),
                pltpu.SMEM((1,), jnp.int32),
                dma(()),
                dma((heads,)),
                dma((heads,)),
                dma(()),
                dma((2,)),
                dma((lines,)),
                dma(()),
                dma(()),
                dma(()),
                dma(()),
                dma((2,)),
                pltpu.SemaphoreType.REGULAR,
            ],
            compiler_params=pltpu.CompilerParams(
                collective_id=0, has_side_effects=True, vmem_limit_bytes=58 * 1024 * 1024
            ),
        )(
            text_block,
            text_length,
            video_query,
            video_key,
            video_value,
            cross_query,
            text_rows,
            key_weight,
            value_weight,
        )
    )


def solution(mesh):
    return jax.shard_map(
        body,
        mesh=mesh,
        in_specs=(
            P(("clip", "seq"), None),
            P(("clip", "seq"), None),
            P(("clip", "seq"), None),
            P(("clip", "seq"), None),
            P(("clip", "seq"), None),
            P("clip"),
            P("clip"),
            P(None, "seq"),
            P(None, "seq"),
        ),
        out_specs=(P(("clip", "seq"), None), P(("clip", "seq"), None)),
        check_vma=False,
    )
```

time: 166 us -> 164 us (0.988)
  no operation moved by 1% of the time
where the time goes in v3:
time: 164 us; the launch traced here: 163 us
  Pallas kernels  162 us (99%)
    pallas_call x1, Pallas kernels, body(): pl.pallas_call(functools.partial(kernel, n, lines), name='video_block', o...  161 us

profile of v3, /device:TPU:12, one launch (start us, length us, event | category | flops | bytes accessed | tf_op | source)
XLA Modules:
  0.0 163.1 jit_solution(12611107951442597125)
XLA Ops:
  1.3 160.5 %video_block.1 = (bf16[128,4096]{1,0:T(8,128)(2,1)S(1)}, bf16[128,4096]{1,0:T(8,128)(2,1)S(1)}) custom-call(s32[8]{0:T(128)} %block_in.1, s32[1]{0:T(128)S(6)} %copy.11.length_in, bf16[128,4096]{1,0:T(8,128)(2,1)} %q_in.1, bf16[128,4096]{1,0:T(8,128)(2,1)} %k_in.1, bf16[128,4096]{1,0:T(8,128)(2,1)} %v_in.1, bf16[128,4096]{1,0:T(8,128)(2,1)} %c_in.1, ...), custom_call_target="tpu_custom_call" | custom-call | tf_op jit(solution)/shard_map/video_block/pallas_call | solution.py:395
  161.8 1.3 settle.1

commit v4 on v3

--- a/solution.py
+++ b/solution.py
@@ -187,14 +187,15 @@
 
     results = (self_out, cross_out)
 
-    def send_out(t, h, late):
+    def send_out(t, h, stages):
         source, landing = made.at[t, h], results[t]
 
         def one(d, carry):
             target = (me + d) % n
-            last = jnp.logical_and(far(target), target // side % 2 == 1)
-
-            @pl.when(last if late else jnp.logical_not(last))
+            stage = jnp.where(far(target), target // side % split + target % side, 0)
+            now = functools.reduce(jnp.logical_or, [stage == k for k in stages])
+
+            @pl.when(now)
             def _():
                 pltpu.make_async_remote_copy(
                     src_ref=source.at[rows(target), :],
@@ -208,19 +209,20 @@
             return carry
 
         lax.fori_loop(1, n, one, 0)
-        if not late:
+        if 0 in stages:
             pltpu.make_async_copy(
                 source.at[rows(me), :], landing.at[:, columns(me, h)], out_recv.at[t]
             ).start()
 
     block = math.gcd(tokens, 256)
+    stages = split + side - 1
 
     def self_head(h):
         arrived = taken.at[h, pl.ds(0, 3)]
         pltpu.make_async_copy(arrived, arrived, qkv_recv.at[h]).wait()
         attend(taken.at[h, 0], taken.at[h, 1], taken.at[h, 2], None, made.at[0, h], block)
-        send_out(0, h, False)
-        send_out(0, h, True)
+        for stage in range(stages):
+            send_out(0, h, (stage,))
 
     @pl.when(middle)
     def _():
@@ -321,9 +323,10 @@
         arrived = taken.at[h, 3]
         pltpu.make_async_copy(arrived, arrived, c_recv.at[h]).wait()
         attend(arrived, tk.at[:, c], tv.at[:, c], bias, made.at[1, h], block)
-        send_out(1, h, False)
-    for h in range(heads):
-        send_out(1, h, True)
+        send_out(1, h, (0,))
+    for stage in range(1, stages):
+        for h in range(heads):
+            send_out(1, h, (stage,))
 
     away = pl.ds(0, (n - 1) * own)
     part = taken.at[:, :, away, :]

time: 164 us -> 163 us (level)
  no operation moved by 1% of the time
where the time goes in v4:
time: 163 us
  Pallas kernels  162 us (99%)
    pallas_call x1, Pallas kernels, body(): pl.pallas_call(functools.partial(kernel, n, lines), name='video_block', o...  160 us

profile of v4, /device:TPU:12, one launch (start us, length us, event | category | flops | bytes accessed | tf_op | source)
XLA Modules:
  0.0 163.1 jit_solution(4769109423614483038)
XLA Ops:
  1.3 160.4 %video_block.1 = (bf16[128,4096]{1,0:T(8,128)(2,1)S(1)}, bf16[128,4096]{1,0:T(8,128)(2,1)S(1)}) custom-call(s32[8]{0:T(128)} %block_in.1, s32[1]{0:T(128)S(6)} %copy.11.length_in, bf16[128,4096]{1,0:T(8,128)(2,1)} %q_in.1, bf16[128,4096]{1,0:T(8,128)(2,1)} %k_in.1, bf16[128,4096]{1,0:T(8,128)(2,1)} %v_in.1, bf16[128,4096]{1,0:T(8,128)(2,1)} %c_in.1, ...), custom_call_target="tpu_custom_call" | custom-call | tf_op jit(solution)/shard_map/video_block/pallas_call | solution.py:398
  161.7 1.3 settle.1

commit v5 on v4

--- a/solution.py
+++ b/solution.py
@@ -221,18 +221,22 @@
         arrived = taken.at[h, pl.ds(0, 3)]
         pltpu.make_async_copy(arrived, arrived, qkv_recv.at[h]).wait()
         attend(taken.at[h, 0], taken.at[h, 1], taken.at[h, 2], None, made.at[0, h], block)
-        for stage in range(stages):
-            send_out(0, h, (stage,))
+        send_out(0, h, range(stages))
 
     @pl.when(middle)
     def _():
         hail(barrier, low + high - pos, lane)
         own_text.start()
+
+        @pl.when(pos == low)
+        def _():
+            line_wait(pos)
+
         pl.semaphore_wait(barrier, 1)
 
         @pl.when(pos == low)
         def _():
-            forward_up(text_in, pos)
+            forward_up(text.at[me], pos)
 
         @pl.when(pos == high)
         def _():
@@ -285,7 +289,10 @@
     for h in range(max(lines, heads) - 1, heads):
         self_head(h)
 
-    line_wait(pos)
+    @pl.when(pos != low)
+    def _():
+        line_wait(pos)
+
     if side > 1:
         others = text.at[pl.ds(0, n - lines)]
         pltpu.make_async_copy(others, others, side_recv).wait()

time: 163 us -> 163 us (level)
  no operation moved by 1% of the time
where the time goes in v5:
time: 163 us
  Pallas kernels  162 us (99%)
    pallas_call x1, Pallas kernels, body(): pl.pallas_call(functools.partial(kernel, n, lines), name='video_block', o...  160 us

profile of v5, /device:TPU:12, one launch (start us, length us, event | category | flops | bytes accessed | tf_op | source)
XLA Modules:
  0.0 163.0 jit_solution(17481397995608958929)
XLA Ops:
  1.3 160.4 %video_block.1 = (bf16[128,4096]{1,0:T(8,128)(2,1)S(1)}, bf16[128,4096]{1,0:T(8,128)(2,1)S(1)}) custom-call(s32[8]{0:T(128)} %block_in.1, s32[1]{0:T(128)S(6)} %copy.11.length_in, bf16[128,4096]{1,0:T(8,128)(2,1)} %q_in.1, bf16[128,4096]{1,0:T(8,128)(2,1)} %k_in.1, bf16[128,4096]{1,0:T(8,128)(2,1)} %v_in.1, bf16[128,4096]{1,0:T(8,128)(2,1)} %c_in.1, ...), custom_call_target="tpu_custom_call" | custom-call | tf_op jit(solution)/shard_map/video_block/pallas_call | solution.py:405
  161.7 1.3 settle.1

commit v6 on v5

--- a/solution.py
+++ b/solution.py
@@ -331,9 +331,11 @@
         pltpu.make_async_copy(arrived, arrived, c_recv.at[h]).wait()
         attend(arrived, tk.at[:, c], tv.at[:, c], bias, made.at[1, h], block)
         send_out(1, h, (0,))
-    for stage in range(1, stages):
-        for h in range(heads):
-            send_out(1, h, (stage,))
+    for step in range(heads + stages):
+        for stage in range(1, stages):
+            h = step - 2 * (stage - 1)
+            if 0 <= h < heads:
+                send_out(1, h, (stage,))
 
     away = pl.ds(0, (n - 1) * own)
     part = taken.at[:, :, away, :]

time: 163 us -> 163 us (level)
  no operation moved by 1% of the time
where the time goes in v6:
time: 163 us
  Pallas kernels  162 us (99%)
    pallas_call x1, Pallas kernels, body(): pl.pallas_call(functools.partial(kernel, n, lines), name='video_block', o...  160 us

profile of v6, /device:TPU:12, one launch (start us, length us, event | category | flops | bytes accessed | tf_op | source)
XLA Modules:
  0.0 163.0 jit_solution(13500324800353798466)
XLA Ops:
  1.3 160.4 %video_block.1 = (bf16[128,4096]{1,0:T(8,128)(2,1)S(1)}, bf16[128,4096]{1,0:T(8,128)(2,1)S(1)}) custom-call(s32[8]{0:T(128)} %block_in.1, s32[1]{0:T(128)S(6)} %copy.11.length_in, bf16[128,4096]{1,0:T(8,128)(2,1)} %q_in.1, bf16[128,4096]{1,0:T(8,128)(2,1)} %k_in.1, bf16[128,4096]{1,0:T(8,128)(2,1)} %v_in.1, bf16[128,4096]{1,0:T(8,128)(2,1)} %c_in.1, ...), custom_call_target="tpu_custom_call" | custom-call | tf_op jit(solution)/shard_map/video_block/pallas_call | solution.py:407
  161.7 1.3 settle.1

commit v7 on v6

--- a/solution.py
+++ b/solution.py
@@ -165,18 +165,28 @@
     def rows(owner):
         return pl.ds(pl.multiple_of(owner * own, own), own)
 
-    def send_in(which, h, recv):
+    ahead = jnp.logical_and(pos == low, lane != 0)
+
+    def send_block(which, h, recv, target):
+        for t in which:
+            pltpu.make_async_remote_copy(
+                src_ref=sources[t].at[:, columns(target, h)],
+                dst_ref=taken.at[h, t, rows(me), :],
+                send_sem=in_send,
+                recv_sem=recv.at[h],
+                device_id=to(target),
+                device_id_type=MESH,
+            ).start()
+
+    def send_in(which, h, recv, held=False):
         def one(d, carry):
             target = (me + d) % n
-            for t in which:
-                pltpu.make_async_remote_copy(
-                    src_ref=sources[t].at[:, columns(target, h)],
-                    dst_ref=taken.at[h, t, rows(me), :],
-                    send_sem=in_send,
-                    recv_sem=recv.at[h],
-                    device_id=to(target),
-                    device_id_type=MESH,
-                ).start()
+            sent = jnp.logical_and(held, target == high * side)
+
+            @pl.when(jnp.logical_not(sent))
+            def _():
+                send_block(which, h, recv, target)
+
             return carry
 
         for t in which:
@@ -225,7 +235,15 @@
 
     @pl.when(middle)
     def _():
-        hail(barrier, low + high - pos, lane)
+        @pl.when(pos == low)
+        def _():
+            hail(barrier, high, lane)
+
+        @pl.when(jnp.logical_and(pos == high, lane == 0))
+        def _():
+            for k in range(side):
+                hail(barrier, low, k)
+
         own_text.start()
 
         @pl.when(pos == low)
@@ -233,6 +251,15 @@
             line_wait(pos)
 
         pl.semaphore_wait(barrier, 1)
+
+        @pl.when(jnp.logical_and(pos == high, lane != 0))
+        def _():
+            hail(ready, low, lane)
+
+        @pl.when(ahead)
+        def _():
+            send_block((0, 1, 2), 0, qkv_recv, high * side)
+            pl.semaphore_wait(ready, 1)
 
         @pl.when(pos == low)
         def _():
@@ -273,7 +300,7 @@
         forward_down(text_in, pos)
 
     forward_side(text_in, pos)
-    send_in((0, 1, 2), 0, qkv_recv)
+    send_in((0, 1, 2), 0, qkv_recv, ahead)
     for copy in loads:
         copy.start()
     for step in range(1, max(lines, heads)):

time: 163 us -> 163 us (level)
  no operation moved by 1% of the time
where the time goes in v7:
time: 163 us
  Pallas kernels  162 us (99%)
    pallas_call x1, Pallas kernels, body(): pl.pallas_call(functools.partial(kernel, n, lines), name='video_block', o...  160 us

profile of v7, /device:TPU:12, one launch (start us, length us, event | category | flops | bytes accessed | tf_op | source)
XLA Modules:
  0.0 163.0 jit_solution(2023161261212190718)
XLA Ops:
  1.3 160.4 %video_block.1 = (bf16[128,4096]{1,0:T(8,128)(2,1)S(1)}, bf16[128,4096]{1,0:T(8,128)(2,1)S(1)}) custom-call(s32[8]{0:T(128)} %block_in.1, s32[1]{0:T(128)S(6)} %copy.11.length_in, bf16[128,4096]{1,0:T(8,128)(2,1)} %q_in.1, bf16[128,4096]{1,0:T(8,128)(2,1)} %k_in.1, bf16[128,4096]{1,0:T(8,128)(2,1)} %v_in.1, bf16[128,4096]{1,0:T(8,128)(2,1)} %c_in.1, ...), custom_call_target="tpu_custom_call" | custom-call | tf_op jit(solution)/shard_map/video_block/pallas_call | solution.py:434
  161.7 1.3 settle.1
